TPU v7x, 256 devices: a whole 4x4x8 slice. The times are simulated.
256 devices in a mesh: dp: 64 (over z, x, core), head: 4 (over y).
Axes of the slice: x: 4, y: 4, z: 8, core: 2. Of those that a mesh axis runs over, the one named last changes fastest.
Arguments:
- queries: bfloat16 [32768, 2048], P('dp', 'head'), may hold values from -48 to 48
- encodings: bfloat16 [1024, 128, 896], P('dp', None, 'head'), may hold values from -12 to 12
- neighbour_ids: int32 [512, 2], P('dp'), may hold values from 0 to 1023, as said below
- block_place: int32 [1024], replicated, may hold values from 0 to 1023, as said below
- query_weight: bfloat16 [4096, 2048], P(None, 'head'), may hold values from -1 to 1
- key_weight: bfloat16 [896, 2048], P(None, 'head'), may hold values from -1 to 1
- value_weight: bfloat16 [896, 2048], P(None, 'head'), may hold values from -0.1875 to 0.1875
- attn_grad: bfloat16 [32768, 2048], P('dp', 'head'), may hold values from -24 to 24
Outputs:
- query_input_grad: bfloat16 [32768, 4096], P('dp', 'head')
- encodings_grad: bfloat16 [1024, 128, 896], P('dp', None, 'head')
- key_weight_grad: float32 [896, 2048], P('dp', 'head')
- value_weight_grad: float32 [896, 2048], P('dp', 'head')
Inputs may be any that keep to these rules, and one draw needn't show every extreme that they name: `neighbour_ids`: block b is stored at position block_place[b] of encodings, on the index block_place[b] // 16 of dp. Of the 16 slots of the spans of one index of dp, each index of dp stores the blocks of 1 or 0, and some index stores those of exactly 1. `block_place`: A permutation: every position once.
All inputs are finite; a program needn't handle non-finite values.
Results may differ from a plain program's by a relative error of at most 0.012.
The roundings to bfloat16 on the way count: a program that leaves them out, or rounds other values in their place, can miss the bound.
Values may be sent and summed in bfloat16 or wider, within the bound.
No kernel may reach another device: no remote copies, remote signals or barrier semaphores. Data moves between devices by JAX's collectives and lax.ppermute only.
A program may use at most 128 MiB of HBM per device.

v0:
```python
import math
import jax
import jax.numpy as jnp
from jax import lax
from jax.sharding import PartitionSpec as P

DH = 128
E = 896
CH = 64
NTOK = 128
NEIGH = 2


def shards(
    queries,
    encodings,
    neighbour_ids,
    block_place,
    query_weight,
    key_weight,
    value_weight,
    attn_grad,
):
    dp_count = lax.axis_size("dp")
    own_blocks = encodings.shape[0]
    span_count = neighbour_ids.shape[0]
    block_names = neighbour_ids.reshape(-1)
    slot_count = block_names.shape[0]
    capacity = -(-slot_count // dp_count)
    position = block_place[block_names]
    owner_dev = position // own_blocks
    local_slot = position % own_blocks
    slot_order = jnp.arange(slot_count, dtype=jnp.int32)
    same_owner = (owner_dev[:, None] == owner_dev[None, :]) & (
        slot_order[None, :] < slot_order[:, None]
    )
    slot_rank = jnp.sum(same_owner.astype(jnp.int32), axis=1)
    device_match = owner_dev[:, None, None] == jnp.arange(dp_count, dtype=jnp.int32)[None, :, None]
    rank_match = slot_rank[:, None, None] == jnp.arange(capacity, dtype=jnp.int32)[None, None, :]
    requests = (
        jnp.sum(jnp.where(device_match & rank_match, local_slot[:, None, None] + 1, 0), axis=0) - 1
    )
    asked_rows = lax.all_to_all(requests, "dp", split_axis=0, concat_axis=0, tiled=True)
    valid_mask = asked_rows >= 0
    local_index = jnp.maximum(asked_rows, 0)
    blank = jnp.zeros((), jnp.bfloat16)
    whole_own = lax.all_gather(encodings, "head", axis=2, tiled=True)
    packed = jnp.where(valid_mask[:, :, None, None], whole_own[local_index], blank)
    received = lax.all_to_all(packed, "dp", split_axis=0, concat_axis=0, tiled=True)
    slot_blocks = received[owner_dev, slot_rank]
    flat_rows = slot_blocks.reshape(-1, E)
    both_weights = jnp.concatenate([key_weight, value_weight], axis=1)
    head_cols = key_weight.shape[1]
    local_heads = head_cols // DH
    projected = jnp.dot(flat_rows, both_weights, preferred_element_type=jnp.float32).astype(
        jnp.bfloat16
    )
    key_rows = projected[:, :head_cols].reshape(span_count, NEIGH * NTOK, local_heads, DH)
    value_rows = projected[:, head_cols:].reshape(span_count, NEIGH * NTOK, local_heads, DH)
    query_heads = queries.reshape(span_count, CH, local_heads, DH)
    grad_heads = attn_grad.reshape(span_count, CH, local_heads, DH)
    score_scale = 1.0 / math.sqrt(DH)
    scores = (
        jnp.einsum("cqhd,ckhd->chqk", query_heads, key_rows, preferred_element_type=jnp.float32)
        * score_scale
    )
    shifted = jnp.exp(scores - jnp.max(scores, axis=-1, keepdims=True))
    prob_rows = shifted / jnp.sum(shifted, axis=-1, keepdims=True)
    prob_half = prob_rows.astype(jnp.bfloat16)
    grad_probs = jnp.einsum(
        "cqhd,ckhd->chqk", grad_heads, value_rows, preferred_element_type=jnp.float32
    )
    row_delta = jnp.sum(prob_rows * grad_probs, axis=-1, keepdims=True)
    grad_scores = (prob_rows * (grad_probs - row_delta) * score_scale).astype(jnp.bfloat16)
    value_grad = jnp.einsum(
        "chqk,cqhd->ckhd", prob_half, grad_heads, preferred_element_type=jnp.float32
    ).astype(jnp.bfloat16)
    key_grad = jnp.einsum(
        "chqk,cqhd->ckhd", grad_scores, query_heads, preferred_element_type=jnp.float32
    ).astype(jnp.bfloat16)
    query_grad = jnp.einsum(
        "chqk,ckhd->cqhd", grad_scores, key_rows, preferred_element_type=jnp.float32
    ).astype(jnp.bfloat16)
    partial_input = jnp.dot(
        query_grad.reshape(-1, head_cols), query_weight.T, preferred_element_type=jnp.float32
    )
    query_input_grad = lax.psum_scatter(
        partial_input.astype(jnp.bfloat16), "head", scatter_dimension=1, tiled=True
    )
    both_grads = jnp.concatenate(
        [key_grad.reshape(-1, head_cols), value_grad.reshape(-1, head_cols)], axis=1
    )
    weight_grads = lax.psum_scatter(
        lax.dot_general(
            flat_rows, both_grads, (((0,), (0,)), ((), ())), preferred_element_type=jnp.float32
        ),
        "dp",
        scatter_dimension=0,
        tiled=True,
    )
    slot_partial = jnp.dot(both_grads, both_weights.T, preferred_element_type=jnp.float32).reshape(
        slot_count, NTOK, E
    )
    slot_grad = lax.psum_scatter(
        slot_partial.astype(jnp.bfloat16), "head", scatter_dimension=2, tiled=True
    )
    quarter = slot_grad.shape[2]
    outgoing = (
        jnp.zeros((dp_count, capacity, NTOK, quarter), jnp.bfloat16)
        .at[owner_dev, slot_rank]
        .set(slot_grad)
    )
    returned = lax.all_to_all(outgoing, "dp", split_axis=0, concat_axis=0, tiled=True)
    block_match = (
        local_index.reshape(-1)[None, :] == jnp.arange(own_blocks, dtype=jnp.int32)[:, None]
    )
    target = (block_match & valid_mask.reshape(-1)[None, :]).astype(jnp.bfloat16)
    encodings_grad = jnp.dot(
        target, returned.reshape(dp_count * capacity, -1), preferred_element_type=jnp.float32
    )
    encodings_grad = encodings_grad.reshape(own_blocks, NTOK, quarter).astype(jnp.bfloat16)
    return (
        query_input_grad,
        encodings_grad,
        weight_grads[:, :head_cols],
        weight_grads[:, head_cols:],
    )


def solution(mesh):
    in_specs = (
        P("dp", "head"),
        P("dp", None, "head"),
        P("dp", None),
        P(),
        P(None, "head"),
        P(None, "head"),
        P(None, "head"),
        P("dp", "head"),
    )
    out_specs = (P("dp", "head"), P("dp", None, "head"), P("dp", "head"), P("dp", "head"))
    return jax.shard_map(shards, mesh=mesh, in_specs=in_specs, out_specs=out_specs, check_vma=False)
```

profile of v0, /device:TPU:1, one launch (start us, length us, event | category | flops | bytes accessed | tf_op | source)
XLA Modules:
  0.0 850.1 jit_solution(8906431637875091830)
XLA Ops:
  11.0 22.2 %all_to_all.16 = s32[64,1,1]{2,1,0:T(1,128)S(1)} all-to-all(s32[64,1,1]{2,1,0:T(1,128)S(1)} %copy.110), channel_id=1, replica_groups=mesh['dp'=64,'head'=4] {'dp'}, dimensions={0} | all-to-all | bytes 512 | tf_op jit(solution)/shard_map/all_to_all | solution.py:43
  35.6 24.8 %all-gather.2.cloned.1.call-done = bf16[16,128,896]{1,0,2:T(8,128)(2,1)} async-done(((bf16[16,128,224]{1,0,2:T(8,128)(2,1)}), bf16[16,128,896]{1,0,2:T(8,128)(2,1)}) %all-gather.2.cloned.1.call-update) | async-done | bytes 3670032 | tf_op jit(solution)/shard_map/all_gather | solution.py:47
  60.5 6.5 copy.112
  66.9 10.0 %gather_fusion.1 = bf16[64,128,896]{2,1,0:T(8,128)(2,1)} fusion(bf16[16,128,896]{2,1,0:T(8,128)(2,1)} %copy.112, s32[1024]{0:T(1024)S(1)} %pad_clamp_fusion), kind=kCustom, calls=%fused_computation.1 | custom fusion | bytes 29360384 | tf_op jit(solution)/shard_map/gather | solution.py:48
  76.9 13.5 %fusion.2 = bf16[64,1,128,896]{3,2,1,0:T(8,128)(2,1)} fusion(bf16[64,128,896]{2,1,0:T(8,128)(2,1)} %gather_fusion.1, pred[64]{0:T(512)(128)(4,1)S(1)} %compare_reduce_fusion), kind=kLoop, calls=%fused_computation.7 | loop fusion | flops 7340032 | bytes 29360192 | tf_op jit(solution)/shard_map/jit(_where)/select_n | solution.py:48
  90.4 11.3 %all-to-all-start.1 = ((bf16[64,1,128,896]{3,2,1,0:T(8,128)(2,1)}), bf16[64,1,128,896]{3,2,1,0:T(8,128)(2,1)}, u32[]{:S(2)}, u32[]{:S(2)}) async-start(bf16[64,1,128,896]{3,2,1,0:T(8,128)(2,1)} %fusion.2), calls=%async_computation.1 | async-start | bytes 29360128 | tf_op jit(solution)/shard_map/all_to_all | solution.py:49
  104.8 317.0 %all-to-all-done.1 = bf16[64,1,128,896]{3,2,1,0:T(8,128)(2,1)} async-done(((bf16[64,1,128,896]{3,2,1,0:T(8,128)(2,1)}), bf16[64,1,128,896]{3,2,1,0:T(8,128)(2,1)}, u32[]{:S(2)}, u32[]{:S(2)}) %all-to-all-start.1) | async-done | bytes 14680096 | tf_op jit(solution)/shard_map/all_to_all | solution.py:49
  421.8 8.1 gather_fusion.2
  429.9 6.9 convolution_convert_fusion.1
  452.4 7.9 convert_bitcast_fusion
  460.3 17.2 %convert_bitcast_fusion.1 = bf16[8,256,4,128]{3,1,2,0:T(8,128)(2,1)} fusion(f32[8,4,256,64]{2,3,1,0:T(8,128)} %fusion.8, bf16[8,64,4,128]{3,2,1,0:T(4,128)(2,1)S(1)} %reshape.340, f32[8,4,64,256]{3,2,1,0:T(8,128)} %get-tuple-element.41, f32[8,4,64]{2,1,0:T(4,128)S(1)} %get-tuple-element.40), kind=kOutput, calls=%fused_computation.23 | convolution fusion | flops 138938624 | bytes 6823936 | tf_op jit(solution)/shard_map/chqk,cqhd->ckhd/dot_general | solution.py:78
  494.6 6.2 convolution_convert_fusion.2
  500.8 6.1 copy.124
  506.9 9.1 %fusion.54 = f32[896,1024]{1,0:T(8,128)} fusion(bf16[2048,896]{1,0:T(8,128)(2,1)} %bitcast.125, bf16[2048,1024]{0,1:T(8,128)(2,1)} %copy-done.5), kind=kOutput, calls=%fused_computation.90 | convolution fusion | flops 3758096384 | bytes 11534336 | tf_op jit(solution)/shard_map/dot_general | solution.py:94
  516.1 14.8 %fusion.20 = bf16[8,64,4,128]{3,1,2,0:T(8,128)(2,1)S(1)} fusion(bf16[8,256,4,128]{3,2,1,0:T(4,128)(2,1)S(1)} %reshape.339, f32[8,4,256,64]{2,3,1,0:T(8,128)} %fusion.8, f32[8,4,64,256]{3,2,1,0:T(8,128)} %get-tuple-element.41, f32[8,4,64]{2,1,0:T(4,128)S(1)} %get-tuple-element.40), kind=kOutput, calls=%fused_computation.31 | convolution fusion | flops 138152192 | bytes 6823936 | tf_op jit(solution)/shard_map/chqk,ckhd->cqhd/dot_general | solution.py:81
  531.4 6.5 convolution_convert_fusion
  537.9 15.2 %reduce-scatter.5.cloned.1.call-done = bf16[16,128,224]{1,2,0:T(8,128)(2,1)} async-done(((bf16[16,128,896]{1,2,0:T(8,128)(2,1)}), bf16[16,128,224]{1,2,0:T(8,128)(2,1)}) %reduce-scatter.5.cloned.1.call-update) | async-done | bytes 917520 | tf_op jit(solution)/shard_map/reduce_scatter | solution.py:104
  558.4 11.0 %all-to-all-start.2 = ((bf16[64,1,128,224]{2,3,1,0:T(8,128)(2,1)}), bf16[64,1,128,224]{2,3,1,0:T(8,128)(2,1)}, u32[]{:S(2)}, u32[]{:S(2)}) async-start(bf16[64,1,128,224]{2,3,1,0:T(8,128)(2,1)} %bitcast.117), calls=%async_computation.4 | async-start | bytes 7340032 | tf_op jit(solution)/shard_map/all_to_all | solution.py:113
  570.6 219.8 %all-reduce.3.cloned.1.call-done = f32[896,1024]{1,0:T(8,128)} async-done(((f32[896,1024]{1,0:T(8,128)}), f32[896,1024]{1,0:T(8,128)}) %all-reduce.3.cloned.1.call-update) | async-done | bytes 3670032
  791.9 6.2 copy.126
  798.1 9.7 %reshape.346 = bf16[64,28672]{1,0:T(8,128)(2,1)} reshape(bf16[64,1,128,224]{3,2,0,1:T(8,128)(2,1)} %copy.126) | data formatting | bytes 7340032 | tf_op jit(solution)/shard_map/reshape | solution.py:119
  807.8 8.0 dot_general.46
  815.9 6.6 copy.127
  826.3 16.9 %reduce-scatter.3.cloned.1.call-done = bf16[512,1024]{1,0:T(8,128)(2,1)} async-done(((bf16[512,4096]{1,0:T(8,128)(2,1)}), bf16[512,1024]{1,0:T(8,128)(2,1)}) %reduce-scatter.3.cloned.1.call-update) | async-done | bytes 1048592 | tf_op jit(solution)/shard_map/reduce_scatter | solution.py:87
  (76 shorter events, 53.6 us)
Async XLA Ops:
  7.2 2.7 copy-start
  7.2 2.5 copy-start.12
  7.2 53.3 %all-gather.2.cloned.1.call-start = ((), (), s32[]{:S(2)}) async-start(), calls=%async_computation.5 | async-start | bytes 4587520 | tf_op jit(solution)/shard_map/all_gather | solution.py:47
  90.4 11.4 %copy-start.8 = (bf16[512,512]{1,0:T(8,128)(2,1)S(1)}, bf16[512,512]{1,0:T(8,128)(2,1)}, u32[]{:S(2)}) copy-start(bf16[512,512]{1,0:T(8,128)(2,1)} %param.8) | copy-start | bytes 1572868
  90.4 331.4 %all-to-all-start.1 = ((bf16[64,1,128,896]{3,2,1,0:T(8,128)(2,1)}), bf16[64,1,128,896]{3,2,1,0:T(8,128)(2,1)}, u32[]{:S(2)}, u32[]{:S(2)}) async-start(bf16[64,1,128,896]{3,2,1,0:T(8,128)(2,1)} %fusion.2), calls=%async_computation.1 | async-start | bytes 29360128 | tf_op jit(solution)/shard_map/all_to_all | solution.py:49
  101.7 1.5 copy-start.6
  101.8 1.6 copy-start.7
  101.8 451.4 %reduce-scatter.5.cloned.1.call-start = ((), (), s32[]{:S(2)}) async-start(), calls=%async_computation.7 | async-start | bytes 4587520 | tf_op jit(solution)/shard_map/reduce_scatter | solution.py:104
  103.5 1.3 copy-start.9
  421.8 8.1 copy-start.10
  442.5 2.2 copy-start.2
  490.3 2.8 copy-start.4
  493.1 1.5 copy-start.11
  494.6 6.2 copy-start.5
  506.9 283.5 %all-reduce.3.cloned.1.call-start = ((), (), s32[]{:S(2)}) async-start(), calls=%async_computation.8 | async-start | bytes 7340032
  516.1 327.1 %reduce-scatter.3.cloned.1.call-start = ((), (), s32[]{:S(2)}) async-start(), calls=%async_computation.6 | async-start | bytes 5242880 | tf_op jit(solution)/shard_map/reduce_scatter | solution.py:87
  553.1 2.3 copy-start.3
  558.4 11.0 %copy-start.13 = (u32[256]{0:T(256)S(1)}, u32[256]{0:T(256)}, u32[]{:S(2)}) copy-start(u32[256]{0:T(256)} %constant.70) | copy-start | bytes 3076
  558.4 233.5 %all-to-all-start.2 = ((bf16[64,1,128,224]{2,3,1,0:T(8,128)(2,1)}), bf16[64,1,128,224]{2,3,1,0:T(8,128)(2,1)}, u32[]{:S(2)}, u32[]{:S(2)}) async-start(bf16[64,1,128,224]{2,3,1,0:T(8,128)(2,1)} %bitcast.117), calls=%async_computation.4 | async-start | bytes 7340032 | tf_op jit(solution)/shard_map/all_to_all | solution.py:113
  815.9 27.4 %copy-start.1 = (s32[1024]{0:T(1024)S(1)}, s32[1024]{0:T(1024)}, u32[]{:S(2)}) copy-start(s32[1024]{0:T(1024)} %param.11) | copy-start | bytes 12292
Sparse Core Ops, SparseCore 0:
  10.4 50.0 all-gather.1
  507.0 46.1 reduce-scatter.4
  556.7 233.6 all-reduce.2
  793.3 49.8 reduce-scatter.2
where the time goes:
time: 857 us; the launch traced here: 850 us
  waiting for transfers between devices  594 us (69%)
  local copies, waits for them, and re-layouts  102 us (12%)
  matrix products  76 us (9%)
  starting transfers between devices  22.5 us (3%)
  blocking collectives  22.2 us (3%)
  other arithmetic  18.5 us (2%)
  between operations  15 us (2%)
    all_to_all x1, waiting for transfers between devices, shards(): lax.all_to_all(packed, 'dp', split_axis=0, concat_axis=0, tiled=True)  317 us
    unnamed x5, waiting for transfers between devices  220 us
    all_gather x1, waiting for transfers between devices, shards(): whole_own = lax.all_gather(encodings, 'head', axis=2, tiled=True)  24.8 us
    all_to_all x1, blocking collectives, shards(): lax.all_to_all(requests, 'dp', split_axis=0, concat_axis=0, tiled=True)  22.2 us
    dot_general x1, matrix products, shards(): jnp.einsum('chqk,cqhd->ckhd', grad_scores, query_heads, preferred_element...  17.2 us
  transfers between devices with their start and end apart: 6, of which 5 were waited for; matrix products, arithmetic and copies ran while one was open for 9% of the time, Pallas kernels for 0%

commit v1 on v0

--- a/solution.py
+++ b/solution.py
@@ -44,7 +44,9 @@
     valid_mask = asked_rows >= 0
     local_index = jnp.maximum(asked_rows, 0)
     blank = jnp.zeros((), jnp.bfloat16)
-    whole_own = lax.all_gather(encodings, "head", axis=2, tiled=True)
+    whole_own = jnp.concatenate(
+        lax.all_to_all(jnp.stack([encodings] * lax.axis_size("head")), "head", 0, 0), axis=2
+    )
     packed = jnp.where(valid_mask[:, :, None, None], whole_own[local_index], blank)
     received = lax.all_to_all(packed, "dp", split_axis=0, concat_axis=0, tiled=True)
     slot_blocks = received[owner_dev, slot_rank]

time: 857 us -> 812 us (0.947)
  waiting for transfers between devices: 594 us -> 526 us
  local copies, waits for them, and re-layouts: 102 us -> 122 us
    unnamed x5 -> x4, waiting for transfers between devices: 220 us -> 155 us
    all_to_all x0 -> x1, waiting for transfers between devices: none -> 40.2 us  [shards(): lax.all_to_all(jnp.stack([encodings] * lax.axis_size('head')), 'head', 0, 0)]
    all_gather x1 -> x0, waiting for transfers between devices: 24.8 us -> none  [shards(): whole_own = lax.all_gather(encodings, 'head', axis=2, tiled=True)]
    all_to_all x0 -> x2, local copies, waits for them, and re-layouts: none -> 24.2 us  [the longest x1 20 us: shards(): lax.all_to_all(packed, 'dp', split_axis=0, concat_axis=0, tiled=True)]
    reduce_scatter x1, waiting for transfers between devices: 16.9 us -> 0.01 us  [shards(): lax.psum_scatter(partial_input.astype(jnp.bfloat16), 'head', scatter_dime...]
  transfers between devices with their start and end apart: 6 -> 6, of which waited for: 5 -> 4; matrix products, arithmetic and copies ran while one was open for 9% -> 10% of each run, Pallas kernels for 0% -> 0%
where the time goes in v1:
time: 812 us; the launch traced here: 803 us
  waiting for transfers between devices  526 us (65%)
  local copies, waits for them, and re-layouts  122 us (15%)
  matrix products  75.6 us (9%)
  starting transfers between devices  23 us (3%)
  blocking collectives  22.2 us (3%)
  other arithmetic  18.1 us (2%)
  between operations  16.6 us (2%)
    all_to_all x1, waiting for transfers between devices, shards(): lax.all_to_all(packed, 'dp', split_axis=0, concat_axis=0, tiled=True)  316 us
    unnamed x4, waiting for transfers between devices  155 us
    all_to_all x1, waiting for transfers between devices, shards(): lax.all_to_all(jnp.stack([encodings] * lax.axis_size('head')), 'head', 0, 0)  40.2 us
    all_to_all x1, blocking collectives, shards(): lax.all_to_all(requests, 'dp', split_axis=0, concat_axis=0, tiled=True)  22.2 us
    all_to_all x1, local copies, waits for them, and re-layouts, shards(): lax.all_to_all(packed, 'dp', split_axis=0, concat_axis=0, tiled=True)  20 us
    dot_general x1, matrix products, shards(): jnp.einsum('chqk,cqhd->ckhd', grad_scores, query_heads, preferred_element...  17 us
  transfers between devices with their start and end apart: 6, of which 4 were waited for; matrix products, arithmetic and copies ran while one was open for 10% of the time, Pallas kernels for 0%

profile of v1, /device:TPU:1, one launch (start us, length us, event | category | flops | bytes accessed | tf_op | source)
XLA Modules:
  0.0 803.4 jit_solution(2565675848225149839)
XLA Ops:
  9.9 22.2 %all_to_all.21 = s32[64,1,1]{2,1,0:T(1,128)S(1)} all-to-all(s32[64,1,1]{2,1,0:T(1,128)S(1)} %copy.94), channel_id=1, replica_groups=mesh['dp'=64,'head'=4] {'dp'}, dimensions={0} | all-to-all | bytes 512 | tf_op jit(solution)/shard_map/all_to_all | solution.py:43
  35.7 4.7 all-to-all-start.1
  42.9 40.2 %all-to-all-done.1 = bf16[4,16,128,224]{2,3,1,0:T(8,128)(2,1)} async-done(((bf16[4,16,128,224]{2,3,1,0:T(8,128)(2,1)}), bf16[4,16,128,224]{2,3,1,0:T(8,128)(2,1)}, u32[]{:S(2)}, u32[]{:S(2)}) %all-to-all-start.1) | async-done | bytes 3670048 | tf_op jit(solution)/shard_map/all_to_all | solution.py:48
  87.4 9.8 %gather_fusion.1 = bf16[64,128,896]{1,2,0:T(8,128)(2,1)} fusion(bf16[16,128,896]{1,2,0:T(8,128)(2,1)} %bitcast.120, s32[1024]{0:T(1024)S(1)} %pad_clamp_fusion), kind=kCustom, calls=%fused_computation.1 | custom fusion | bytes 29360384 | tf_op jit(solution)/shard_map/gather | solution.py:50
  97.2 13.4 %fusion.2 = bf16[64,1,128,896]{2,3,1,0:T(8,128)(2,1)} fusion(bf16[64,128,896]{1,2,0:T(8,128)(2,1)} %gather_fusion.1, pred[64]{0:T(512)(128)(4,1)S(1)} %compare_reduce_fusion), kind=kLoop, calls=%fused_computation.7 | loop fusion | flops 7340032 | bytes 29360192 | tf_op jit(solution)/shard_map/jit(_where)/select_n | solution.py:50
  110.6 6.8 all-to-all-start.2
  120.5 316.0 %all-to-all-done.2 = bf16[64,1,128,896]{2,3,1,0:T(8,128)(2,1)} async-done(((bf16[64,1,128,896]{2,3,1,0:T(8,128)(2,1)}), bf16[64,1,128,896]{2,3,1,0:T(8,128)(2,1)}, u32[]{:S(2)}, u32[]{:S(2)}) %all-to-all-start.2) | async-done | bytes 14680096 | tf_op jit(solution)/shard_map/all_to_all | solution.py:51
  436.5 20.0 %copy.97 = bf16[64,1,128,896]{3,2,1,0:T(8,128)(2,1)} copy(bf16[64,1,128,896]{2,3,1,0:T(8,128)(2,1)} %all-to-all-done.2) | data formatting | bytes 29360128 | tf_op jit(solution)/shard_map/all_to_all | solution.py:51
  456.5 8.1 %gather_fusion.2 = bf16[16,128,896]{2,1,0:T(8,128)(2,1)} fusion(bf16[64,1,128,896]{3,2,1,0:T(8,128)(2,1)} %copy.97, s32[16]{0:T(128)S(1)} %get-tuple-element.33), kind=kCustom, calls=%fused_computation.2 | custom fusion | bytes 7340160 | tf_op jit(solution)/shard_map/gather | solution.py:52
  464.6 6.8 convolution_convert_fusion.1
  486.8 7.9 convert_bitcast_fusion
  494.7 17.0 %convert_bitcast_fusion.1 = bf16[8,256,4,128]{3,1,2,0:T(8,128)(2,1)} fusion(f32[8,4,256,64]{2,3,1,0:T(8,128)} %fusion.8, bf16[8,64,4,128]{3,2,1,0:T(4,128)(2,1)S(1)} %reshape.350, f32[8,4,64,256]{3,2,1,0:T(8,128)} %get-tuple-element.37, f32[8,4,64]{2,1,0:T(4,128)S(1)} %get-tuple-element.36), kind=kOutput, calls=%fused_computation.23 | convolution fusion | flops 138938624 | bytes 6823936 | tf_op jit(solution)/shard_map/chqk,cqhd->ckhd/dot_general | solution.py:80
  529.0 6.0 convolution_convert_fusion.2
  535.0 6.1 copy.108
  541.2 9.2 %fusion.54 = f32[896,1024]{1,0:T(8,128)} fusion(bf16[2048,896]{1,0:T(8,128)(2,1)} %bitcast.129, bf16[2048,1024]{0,1:T(8,128)(2,1)} %copy-done.5), kind=kOutput, calls=%fused_computation.90 | convolution fusion | flops 3758096384 | bytes 11534336 | tf_op jit(solution)/shard_map/dot_general | solution.py:96
  550.7 14.7 %fusion.20 = bf16[8,64,4,128]{3,1,2,0:T(8,128)(2,1)S(1)} fusion(bf16[8,256,4,128]{3,2,1,0:T(4,128)(2,1)S(1)} %reshape.349, f32[8,4,256,64]{2,3,1,0:T(8,128)} %fusion.8, f32[8,4,64,256]{3,2,1,0:T(8,128)} %get-tuple-element.37, f32[8,4,64]{2,1,0:T(4,128)S(1)} %get-tuple-element.36), kind=kOutput, calls=%fused_computation.31 | convolution fusion | flops 138152192 | bytes 6823936 | tf_op jit(solution)/shard_map/chqk,ckhd->cqhd/dot_general | solution.py:83
  565.9 6.6 convolution_convert_fusion
  572.5 15.2 %reduce-scatter.5.cloned.1.call-done = bf16[16,128,224]{1,2,0:T(8,128)(2,1)} async-done(((bf16[16,128,896]{1,2,0:T(8,128)(2,1)}), bf16[16,128,224]{1,2,0:T(8,128)(2,1)}) %reduce-scatter.5.cloned.1.call-update) | async-done | bytes 917520 | tf_op jit(solution)/shard_map/reduce_scatter | solution.py:106
  592.9 11.1 %all-to-all-start.3 = ((bf16[64,1,128,224]{2,3,1,0:T(8,128)(2,1)}), bf16[64,1,128,224]{2,3,1,0:T(8,128)(2,1)}, u32[]{:S(2)}, u32[]{:S(2)}) async-start(bf16[64,1,128,224]{2,3,1,0:T(8,128)(2,1)} %bitcast.121), calls=%async_computation.5 | async-start | bytes 7340032 | tf_op jit(solution)/shard_map/all_to_all | solution.py:115
  605.2 154.7 %all-reduce.3.cloned.1.call-done = f32[896,1024]{1,0:T(8,128)} async-done(((f32[896,1024]{1,0:T(8,128)}), f32[896,1024]{1,0:T(8,128)}) %all-reduce.3.cloned.1.call-update) | async-done | bytes 3670032
  761.5 6.2 copy.110
  767.7 9.7 %reshape.356 = bf16[64,28672]{1,0:T(8,128)(2,1)} reshape(bf16[64,1,128,224]{3,2,0,1:T(8,128)(2,1)} %copy.110) | data formatting | bytes 7340032 | tf_op jit(solution)/shard_map/reshape | solution.py:121
  777.4 8.0 dot_general.46
  785.4 6.5 copy.111
  (74 shorter events, 59.6 us)
Async XLA Ops:
  8.0 0.9 copy-start
  35.7 47.4 %all-to-all-start.1 = ((bf16[4,16,128,224]{2,3,1,0:T(8,128)(2,1)}), bf16[4,16,128,224]{2,3,1,0:T(8,128)(2,1)}, u32[]{:S(2)}, u32[]{:S(2)}) async-start(bf16[4,16,128,224]{2,3,1,0:T(8,128)(2,1)} %stack.2), calls=%async_computation.1 | async-start | bytes 7340032 | tf_op jit(solution)/shard_map/all_to_all | solution.py:48
  110.6 6.9 copy-start.8
  110.6 325.9 %all-to-all-start.2 = ((bf16[64,1,128,896]{2,3,1,0:T(8,128)(2,1)}), bf16[64,1,128,896]{2,3,1,0:T(8,128)(2,1)}, u32[]{:S(2)}, u32[]{:S(2)}) async-start(bf16[64,1,128,896]{2,3,1,0:T(8,128)(2,1)} %fusion.2), calls=%async_computation.2 | async-start | bytes 29360128 | tf_op jit(solution)/shard_map/all_to_all | solution.py:51
  117.5 1.5 copy-start.6
  117.5 1.6 copy-start.7
  117.5 470.2 %reduce-scatter.5.cloned.1.call-start = ((), (), s32[]{:S(2)}) async-start(), calls=%async_computation.7 | async-start | bytes 4587520 | tf_op jit(solution)/shard_map/reduce_scatter | solution.py:106
  119.2 1.3 copy-start.9
  456.5 8.1 %copy-start.10 = (bf16[896,1024]{1,0:T(8,128)(2,1)S(1)}, bf16[896,1024]{1,0:T(8,128)(2,1)}, u32[]{:S(2)}) copy-start(bf16[896,1024]{1,0:T(8,128)(2,1)} %copy-done.9) | copy-start | bytes 5505028
  477.1 2.0 copy-start.2
  524.7 2.8 copy-start.4
  527.5 1.5 copy-start.11
  529.0 6.0 copy-start.5
  541.1 218.8 %all-reduce.3.cloned.1.call-start = ((), (), s32[]{:S(2)}) async-start(), calls=%async_computation.8 | async-start | bytes 7340032
  550.4 245.3 %reduce-scatter.3.cloned.1.call-start = ((), (), s32[]{:S(2)}) async-start(), calls=%async_computation.6 | async-start | bytes 5242880 | tf_op jit(solution)/shard_map/reduce_scatter | solution.py:89
  587.6 2.3 copy-start.3
  592.9 11.1 %copy-start.12 = (u32[256]{0:T(256)S(1)}, u32[256]{0:T(256)}, u32[]{:S(2)}) copy-start(u32[256]{0:T(256)} %constant.70) | copy-start | bytes 3076
  592.9 168.6 %all-to-all-start.3 = ((bf16[64,1,128,224]{2,3,1,0:T(8,128)(2,1)}), bf16[64,1,128,224]{2,3,1,0:T(8,128)(2,1)}, u32[]{:S(2)}, u32[]{:S(2)}) async-start(bf16[64,1,128,224]{2,3,1,0:T(8,128)(2,1)} %bitcast.121), calls=%async_computation.5 | async-start | bytes 7340032 | tf_op jit(solution)/shard_map/all_to_all | solution.py:115
  785.4 10.3 %copy-start.1 = (s32[1024]{0:T(1024)S(1)}, s32[1024]{0:T(1024)}, u32[]{:S(2)}) copy-start(s32[1024]{0:T(1024)} %param.11) | copy-start | bytes 12292
Sparse Core Ops, SparseCore 0:
  541.2 46.3 reduce-scatter.4
  590.8 49.1 reduce-scatter.2
Sparse Core Ops, SparseCore 1:
  550.5 209.4 all-reduce.2
